TPU v7x, 128 devices: a whole 4x4x4 slice. The times are simulated.
128 devices in a mesh: dp: 16 (over x, z_hi, core), tensor: 8 (over z_lo, y).
Axes of the slice: x: 4, y: 4, z: 4 (z_hi: 2, z_lo: 2; z = z_hi * 2 + z_lo), core: 2. Of those that a mesh axis runs over, the one named last changes fastest.
Arguments:
- gate_pre: bfloat16 [16384, 7168], P('dp', 'tensor'), may hold values from -6 to 6
- up_pre: bfloat16 [16384, 7168], P('dp', 'tensor'), may hold values from -6 to 6
- down_weight: bfloat16 [7168, 4096], P('tensor'), may hold values from -0.0625 to 0.0625
- grad_out: bfloat16 [16384, 4096], P(('dp', 'tensor')), may hold values from -24 to 24
Outputs:
- ffn_out: bfloat16 [16384, 4096], P(('dp', 'tensor'))
- grad_gate: bfloat16 [16384, 7168], P('dp', 'tensor')
- grad_up: bfloat16 [16384, 7168], P('dp', 'tensor')
- grad_down: float32 [7168, 4096], P('tensor', 'dp')
All inputs are finite; a program needn't handle non-finite values.
Results may differ from a plain program's by a relative error of at most 0.017.
Values may be sent and summed in bfloat16 or wider, within the bound.
A program may use at most 128 MiB of HBM per device.

v0:
```python
import math

import jax
import jax.numpy as jnp
from jax import lax
from jax.sharding import PartitionSpec as P


def body(gate_pre, up_pre, down_weight, grad_out):
    gate_val = gate_pre.astype(jnp.float32)
    up_val = up_pre.astype(jnp.float32)
    sigmoid_gate = jax.nn.sigmoid(gate_val)
    activated = gate_val * sigmoid_gate
    hidden = (activated * up_val).astype(jnp.bfloat16)
    replica_rows = hidden.shape[0]
    grad_scale = 1.0 / math.sqrt(replica_rows * lax.axis_size("dp"))
    hidden_rows = hidden
    ffn_out = lax.psum_scatter(
        jnp.dot(hidden_rows, down_weight, preferred_element_type=jnp.float32).astype(jnp.bfloat16),
        "tensor",
        scatter_dimension=0,
        tiled=True,
    )
    piece = lax.all_gather(grad_out, "tensor", axis=0, tiled=True)
    product = jnp.einsum("td,fd->tf", piece, down_weight, preferred_element_type=jnp.float32)
    hidden_grad = product
    hidden_rows = hidden
    weight_grad = jnp.einsum("tf,td->fd", hidden_rows, piece, preferred_element_type=jnp.float32)
    hidden_grad, weight_grad = (hidden_grad, weight_grad)
    grad_down = lax.psum_scatter(
        (weight_grad * grad_scale).astype(jnp.bfloat16), "dp", scatter_dimension=1, tiled=True
    ).astype(jnp.float32)
    grad_gate = (
        hidden_grad * up_val * sigmoid_gate * (1.0 + gate_val * (1.0 - sigmoid_gate))
    ).astype(jnp.bfloat16)
    grad_up = (hidden_grad * activated).astype(jnp.bfloat16)
    return (ffn_out, grad_gate, grad_up, grad_down)


def solution(mesh):
    return jax.shard_map(
        body,
        mesh=mesh,
        in_specs=(
            P("dp", "tensor"),
            P("dp", "tensor"),
            P("tensor", None),
            P(("dp", "tensor"), None),
        ),
        out_specs=(
            P(("dp", "tensor"), None),
            P("dp", "tensor"),
            P("dp", "tensor"),
            P("tensor", "dp"),
        ),
        check_vma=False,
    )
```

profile of v0, /device:TPU:0, one launch (start us, length us, event | category | flops | bytes accessed | tf_op | source)
XLA Modules:
  0.0 312.0 jit_solution(5632840799988935604)
XLA Ops:
  7.2 0.0 all-gather.2.cloned.1.call-start
  7.2 0.7 all-gather.2.cloned.1.call-update
  7.9 0.0 reduce-scatter.5.cloned.1.call-start
  7.9 96.2 %all-gather.2.cloned.1.call-done = bf16[1024,4096]{1,0:T(8,128)(2,1)} async-done(((bf16[128,4096]{1,0:T(8,128)(2,1)}), bf16[1024,4096]{1,0:T(8,128)(2,1)}) %all-gather.2.cloned.1.call-update) | async-done | bytes 8388624 | tf_op jit(solution)/shard_map/all_gather | solution.py:24
  104.1 13.7 %multiply_convert_fusion = bf16[896,4096]{1,0:T(8,128)(2,1)} fusion(bf16[1024,4096]{1,0:T(8,128)(2,1)} %all-gather.2.cloned.1.call-done, bf16[1024,896]{1,0:T(8,128)(2,1)} %param.5, bf16[1024,896]{1,0:T(8,128)(2,1)} %param.4), kind=kOutput, calls=%fused_computation | convolution fusion | flops 7530872832 | bytes 19398656 | tf_op jit(solution)/shard_map/tf,td->fd/dot_general | solution.py:28
  117.8 0.0 copy-start
  117.8 0.0 reduce-scatter.5.cloned.1.call-update
  117.8 0.2 reduce-scatter.3.cloned.1.call-start
  118.1 1.2 copy-done
  119.3 14.0 %convolution_convert_fusion = bf16[1024,4096]{1,0:T(8,128)(2,1)} fusion(bf16[896,4096]{1,0:T(8,128)(2,1)} %param.6, bf16[1024,896]{1,0:T(8,128)(2,1)S(1)} %copy-done, bf16[1024,896]{1,0:T(8,128)(2,1)} %param.4), kind=kOutput, calls=%fused_computation.1 | convolution fusion | flops 7527727104 | bytes 19398656 | tf_op jit(solution)/shard_map/dot_general | solution.py:19
  133.3 0.0 reduce-scatter.3.cloned.1.call-update
  133.3 17.1 %multiply_convert_fusion.1 = (bf16[1024,896]{1,0:T(8,128)(2,1)}, bf16[1024,896]{1,0:T(8,128)(2,1)}) fusion(bf16[1024,896]{1,0:T(8,128)(2,1)} %param.4, bf16[1024,896]{1,0:T(8,128)(2,1)S(1)} %copy-done, bf16[1024,4096]{1,0:T(8,128)(2,1)} %all-gather.2.cloned.1.call-done, bf16[896,4096]{1,0:T(8,128)(2,1)} %param.6), kind=kOutput, calls=%fused_computation.15 | convolution fusion | flops 7529955328 | bytes 23068672 | tf_op jit(solution)/shard_map/td,fd->tf/dot_general | solution.py:25
  150.4 60.5 %reduce-scatter.5.cloned.1.call-done = bf16[896,256]{1,0:T(8,128)(2,1)} async-done(((bf16[896,4096]{1,0:T(8,128)(2,1)}), bf16[896,256]{1,0:T(8,128)(2,1)}) %reduce-scatter.5.cloned.1.call-update) | async-done | bytes 458768 | tf_op jit(solution)/shard_map/reduce_scatter | solution.py:30
  211.0 2.0 convert_element_type.31
  213.0 92.5 %reduce-scatter.3.cloned.1.call-done = bf16[128,4096]{1,0:T(8,128)(2,1)} async-done(((bf16[1024,4096]{1,0:T(8,128)(2,1)}), bf16[128,4096]{1,0:T(8,128)(2,1)}) %reduce-scatter.3.cloned.1.call-update) | async-done | bytes 1048592 | tf_op jit(solution)/shard_map/reduce_scatter | solution.py:18
Async XLA Ops:
  7.2 97.0 %all-gather.2.cloned.1.call-start = ((), (), s32[]{:S(2)}) async-start(), calls=%async_computation.3 | async-start | bytes 9437184 | tf_op jit(solution)/shard_map/all_gather | solution.py:24
  7.9 203.1 %reduce-scatter.5.cloned.1.call-start = ((), (), s32[]{:S(2)}) async-start(), calls=%async_computation.4 | async-start | bytes 7798784 | tf_op jit(solution)/shard_map/reduce_scatter | solution.py:30
  117.8 1.5 copy-start
  117.8 187.7 %reduce-scatter.3.cloned.1.call-start = ((), (), s32[]{:S(2)}) async-start(), calls=%async_computation.2 | async-start | bytes 9437184 | tf_op jit(solution)/shard_map/reduce_scatter | solution.py:18
Sparse Core Ops, SparseCore 0:
  9.6 94.4 all-gather.1
  117.9 92.9 reduce-scatter.4
  214.1 91.3 reduce-scatter.2
where the time goes:
time: 313 us; the launch traced here: 312 us
  waiting for transfers between devices  250 us (80%)
  matrix products  44.7 us (14%)
  between operations  13.7 us (4%)
    all_gather x1, waiting for transfers between devices, body(): piece = lax.all_gather(grad_out, 'tensor', axis=0, tiled=True)  96.2 us
    reduce_scatter x1, waiting for transfers between devices, body(): lax.psum_scatter(jnp.dot(hidden_rows, down_weight, preferred_element_type...  92.5 us
    reduce_scatter x1, waiting for transfers between devices, body(): lax.psum_scatter((weight_grad * grad_scale).astype(jnp.bfloat16), 'dp', s...  60.5 us
    dot_general x1, matrix products, body(): jnp.einsum('td,fd->tf', piece, down_weight, preferred_element_type=jnp.fl...  17.1 us
    dot_general x1, matrix products, body(): jnp.dot(hidden_rows, down_weight, preferred_element_type=jnp.float32)  14 us
    dot_general x1, matrix products, body(): jnp.einsum('tf,td->fd', hidden_rows, piece, preferred_element_type=jnp.fl...  13.7 us
  transfers between devices with their start and end apart: 3, of which 3 were waited for; matrix products, arithmetic and copies ran while one was open for 11% of the time, Pallas kernels for 0%

commit v1 on v0

v1 whole, which is shorter than its diff:
```python
import functools
import math

import jax
import jax.numpy as jnp
from jax import lax
from jax.experimental import pallas as pl
from jax.experimental.pallas import tpu as pltpu
from jax.sharding import PartitionSpec as P

MESH = pl.DeviceIdType.MESH
F32 = jnp.float32
BF16 = jnp.bfloat16

STEPS = 8
WIDTH = 512
HALF = 256
ROWS = 128
RA = 80
RB = ROWS - RA
FF = 896

LOOKAHEAD = 3
OFF = dict(A1=0, A2=1, A3=2, D1=3, R0=0, R1=1, R2=4, R3=5, R4=6, E=10, D2A=10, D2B=12)
ITERS = 14


def add_rows(dst, srcs, rows):
    def step(t, carry):
        sl = pl.ds(pl.multiple_of(t * 16, 16), 16)
        total = dst[sl, :].astype(F32)
        for src in srcs:
            total += src[sl, :].astype(F32)
        dst[sl, :] = total.astype(dst.dtype)
        return carry

    lax.fori_loop(0, rows // 16, step, 0)


def kernel(
    scale,
    gate_hbm, up_hbm, w_hbm, g_hbm,
    f_out, gg_out, gu_out, gd_out,
    gate_v, up_v, w_v, h_v, ht_v, gb, p, hg,
    rz1, rho, rhw, rfo, rfw, rz2,
    cs, ck, cr, xr, zs, zr, gd_v,
    ag_s, ag_r, rs_s, rs_r, c_s, c_r, x_s, x_r, zh_s, zh_r,
    ld_g, ld_w, ld_a, st_f, st_e, st_d,
):
    dp = lax.axis_index("dp")
    te = lax.axis_index("tensor")
    x, zh, core = dp // 4, (dp // 2) % 2, dp % 2
    z, y = te // 4, te % 4
    yp, ym, y2 = (y + 1) % 4, (y + 3) % 4, (y + 2) % 4
    zo = 1 - z
    own, other = z * 4, zo * 4
    to_yp, to_ym, to_z = (dp, own + yp), (dp, own + ym), (dp, other + y)
    to_core = (x * 4 + zh * 2 + (1 - core), te)
    to_zh = (x * 4 + (1 - zh) * 2 + core, te)

    def to_x(d):
        return (((x + d) % 4) * 4 + zh * 2 + core, te)

    def column(s):
        j = 2 * ((x + 1 + s // 2) % 4) + (s + 1 + zh) % 2
        return pl.ds(pl.multiple_of(j * WIDTH, WIDTH), WIDTH)

    def load_g(s):
        return pltpu.make_async_copy(g_hbm.at[:, column(s)], gb.at[s, te], ld_g.at[s])

    def load_w(s):
        return pltpu.make_async_copy(w_hbm.at[:, column(s)], w_v.at[s], ld_w.at[s])

    load_gate = pltpu.make_async_copy(gate_hbm, gate_v, ld_a.at[0])
    load_up = pltpu.make_async_copy(up_hbm, up_v, ld_a.at[1])

    def each(n, f):
        def step(s, carry):
            f(s)
            return carry

        lax.fori_loop(0, n, step, 0)

    each(STEPS, lambda s: load_g(s).start())
    load_gate.start()
    load_up.start()
    each(STEPS, lambda s: load_w(s).start())

    barrier = pltpu.get_barrier_semaphore()
    for device in (to_yp, to_ym, to_z, to_core, to_zh, to_x(1), to_x(2), to_x(3)):
        pl.semaphore_signal(barrier, inc=1, device_id=device, device_id_type=MESH)
    pl.semaphore_wait(barrier, 8)

    def remote(src, dst, send, recv, device):
        return pltpu.make_async_remote_copy(
            src_ref=src, dst_ref=dst, send_sem=send, recv_sem=recv,
            device_id=device, device_id_type=MESH,
        )

    ROW_ALL, ROW_A, ROW_B = pl.ds(0, ROWS), pl.ds(0, RA), pl.ds(RA, RB)
    COL_ALL, COL_0, COL_1 = pl.ds(0, WIDTH), pl.ds(0, HALF), pl.ds(HALF, HALF)

    gather = (
        (own + y, other + y, ROW_ALL, COL_ALL, to_z),
        (own + y, own + ym, ROW_ALL, COL_ALL, to_yp),
        (own + y, own + yp, ROW_ALL, COL_ALL, to_ym),
        (other + y, other + ym, ROW_A, COL_ALL, to_yp),
        (other + y, other + yp, ROW_A, COL_ALL, to_ym),
        (own + yp, own + y2, ROW_ALL, COL_0, to_ym),
        (own + ym, own + y2, ROW_ALL, COL_1, to_yp),
        (own + yp, other + yp, ROW_B, COL_ALL, to_z),
        (own + ym, other + ym, ROW_B, COL_ALL, to_z),
        (other + yp, other + y2, ROW_A, COL_0, to_ym),
        (other + ym, other + y2, ROW_A, COL_1, to_yp),
        (own + y2, other + y2, ROW_B, COL_0, to_z),
        (own + y2, other + y2, ROW_B, COL_1, to_z),
    )

    def ag(k, s, arriving=False):
        leaves, arrives, rows, cols, device = gather[k]
        ref = gb.at[s, arrives if arriving else leaves, rows, cols]
        return remote(ref, ref, ag_s.at[k, s], ag_r.at[k, s], device)

    def ag_send(k, s):
        ag(k, s).start()

    def ag_wait(k, s):
        ag(k, s, True).wait_recv()

    reduction = (
        (other + yp, ROW_B, COL_ALL, rz1, 0, to_z),
        (other + ym, ROW_B, COL_ALL, rz1, 1, to_z),
        (other + y2, ROW_B, COL_ALL, rz1, 2, to_z),
        (other + y2, ROW_A, COL_0, rho, 0, to_yp),
        (other + y2, ROW_A, COL_1, rho, 1, to_ym),
        (own + y2, ROW_ALL, COL_0, rhw, 0, to_yp),
        (own + y2, ROW_ALL, COL_1, rhw, 1, to_ym),
        (other + yp, ROW_A, COL_ALL, rfo, 0, to_yp),
        (other + ym, ROW_A, COL_ALL, rfo, 1, to_ym),
        (own + yp, ROW_ALL, COL_ALL, rfw, 0, to_yp),
        (own + ym, ROW_ALL, COL_ALL, rfw, 1, to_ym),
        (other + y, ROW_ALL, COL_ALL, rz2, 0, to_z),
    )

    def rs(k, s):
        slot, rows, cols, land, index, device = reduction[k]
        return remote(p.at[s, slot, rows, cols], land.at[s, index], rs_s.at[k, s], rs_r.at[k, s], device)

    def rs_send(k, s):
        rs(k, s).start()

    def rs_wait(k, s):
        rs(k, s).wait_recv()

    def core_copy(s):
        return remote(cs.at[s], cr.at[s], c_s.at[s], c_r.at[s], to_core)

    def x_copy(s):
        return remote(ck.at[s], xr.at[s], x_s.at[s], x_r.at[s], to_x(1 + s // 2))

    zh_copy = remote(zs, zr, zh_s, zh_r, to_zh)

    def a0(s):
        load_g(s).wait()
        for k in (1, 2, 0):
            ag_send(k, s)

    def a1(s):
        ag_wait(0, s)
        ag_send(3, s)
        ag_send(4, s)
        ag_wait(2, s)
        ag_send(5, s)
        ag_send(7, s)
        ag_wait(1, s)
        ag_send(6, s)
        ag_send(8, s)

    def a2(s):
        ag_wait(4, s)
        ag_send(9, s)
        ag_wait(3, s)
        ag_send(10, s)
        ag_wait(5, s)
        ag_send(11, s)
        ag_wait(6, s)
        ag_send(12, s)

    def a3(s):
        for k in range(7, 13):
            ag_wait(k, s)

        def weight_half(side, dst):
            cols = pl.ds(pl.multiple_of(side * HALF, HALF), HALF)

            def tile(t, carry):
                rows = pl.ds(pl.multiple_of(t * 448, 64), 448)
                block = gb[s, :, :, cols].reshape(8 * ROWS, HALF)
                product = jnp.dot(ht_v[rows, :], block, preferred_element_type=F32)
                dst[s, rows, :] = (product * scale).astype(BF16)
                return carry

            lax.fori_loop(0, 2, tile, 0)

        weight_half(1 - core, cs)
        core_copy(s).start()
        weight_half(core, ck)

        def tile(t, carry):
            rows = pl.ds(pl.multiple_of(t * 512, 512), 512)
            block = gb[s, pl.ds(t * 4, 4)].reshape(512, WIDTH)
            product = lax.dot_general(
                block, w_v[s], (((1,), (1,)), ((), ())), preferred_element_type=F32
            )

            @pl.when(s == 0)
            def _():
                hg[rows, :] = product

            @pl.when(s > 0)
            def _():
                hg[rows, :] += product

            return carry

        lax.fori_loop(0, 2, tile, 0)

    def d1(s):
        core_copy(s).wait_recv()
        add_rows(ck.at[s], [cr.at[s]], FF)

        @pl.when(s < 6)
        def _():
            x_copy(s).start()

    def d2a():
        for k in (0, 2, 4):
            x_copy(k).wait_recv()

        def tile(t, carry):
            sl = pl.ds(pl.multiple_of(t * 16, 16), 16)
            total = ck[6, sl, :].astype(F32)
            for k in (0, 2, 4):
                total += xr[k, sl, :].astype(F32)
            zs[sl, :] = total.astype(BF16)
            return carry

        lax.fori_loop(0, FF // 16, tile, 0)
        zh_copy.start()

    save_d = pltpu.make_async_copy(gd_v, gd_out, st_d)

    def d2b():
        for k in (1, 3, 5):
            x_copy(k).wait_recv()
        zh_copy.wait_recv()

        def tile(t, carry):
            sl = pl.ds(pl.multiple_of(t * 16, 16), 16)
            total = ck[7, sl, :].astype(F32) + zr[sl, :].astype(F32)
            for k in (1, 3, 5):
                total += xr[k, sl, :].astype(F32)
            gd_v[sl, :] = total
            return carry

        lax.fori_loop(0, FF // 16, tile, 0)
        save_d.start()

    def r0(s):
        load_w(s).wait()

        def tile(t, carry):
            rows = pl.ds(pl.multiple_of(t * 512, 512), 512)
            product = jnp.dot(h_v[rows, :], w_v[s], preferred_element_type=F32)
            p[s, pl.ds(t * 4, 4)] = product.astype(BF16).reshape(4, ROWS, WIDTH)
            return carry

        lax.fori_loop(0, 2, tile, 0)
        for k in (0, 1, 2, 3, 4):
            rs_send(k, s)

    def r1(s):
        for k, slot in ((2, own + y2), (0, own + yp), (1, own + ym)):
            rs_wait(k, s)
            add_rows(p.at[s, slot, ROW_B, :], [rz1.at[s, k]], RB)
            if k == 2:
                rs_send(5, s)
                rs_send(6, s)

    def r2(s):
        rs_wait(3, s)
        add_rows(p.at[s, other + yp, ROW_A, COL_0], [rho.at[s, 0]], RA)
        rs_send(7, s)
        rs_wait(4, s)
        add_rows(p.at[s, other + ym, ROW_A, COL_1], [rho.at[s, 1]], RA)
        rs_send(8, s)
        rs_wait(5, s)
        add_rows(p.at[s, own + yp, ROW_ALL, COL_0], [rhw.at[s, 0]], ROWS)
        rs_send(9, s)
        rs_wait(6, s)
        add_rows(p.at[s, own + ym, ROW_ALL, COL_1], [rhw.at[s, 1]], ROWS)
        rs_send(10, s)

    def r3(s):
        rs_wait(7, s)
        rs_wait(8, s)
        add_rows(p.at[s, other + y, ROW_A, :], [rfo.at[s, 0], rfo.at[s, 1]], RA)
        rs_send(11, s)

    def save_f(s):
        return pltpu.make_async_copy(p.at[s, te], f_out.at[:, column(s)], st_f.at[s])

    def r4(s):
        for k in (9, 10, 11):
            rs_wait(k, s)
        add_rows(p.at[s, te], [rfw.at[s, 0], rfw.at[s, 1], rz2.at[s, 0]], ROWS)
        save_f(s).start()

    def save_e(e, which):
        rows = pl.ds(pl.multiple_of(e * 256, 256), 256)
        src, dst = ((gate_v, gg_out), (up_v, gu_out))[which]
        return pltpu.make_async_copy(src.at[rows, :], dst.at[rows, :], st_e.at[which, e])

    def e0(e):
        def tile(t, carry):
            sl = pl.ds(pl.multiple_of(e * 256 + t * 16, 16), 16)
            g = gate_v[sl, :].astype(F32)
            u = up_v[sl, :].astype(F32)
            grad = hg[sl, :]
            s = jax.nn.sigmoid(g)
            gate_v[sl, :] = (grad * u * s * (1.0 + g * (1.0 - s))).astype(BF16)
            up_v[sl, :] = (grad * (g * s)).astype(BF16)
            return carry

        lax.fori_loop(0, 16, tile, 0)
        save_e(e, 0).start()
        save_e(e, 1).start()

    each(LOOKAHEAD, a0)
    load_gate.wait()
    load_up.wait()

    def hidden_tile(t, carry):
        sl = pl.ds(pl.multiple_of(t * 16, 16), 16)
        g = gate_v[sl, :].astype(F32)
        u = up_v[sl, :].astype(F32)
        h_v[sl, :] = (g * jax.nn.sigmoid(g) * u).astype(BF16)
        return carry

    lax.fori_loop(0, 64, hidden_tile, 0)

    def transpose_tile(t, carry):
        sl = pl.ds(pl.multiple_of(t * 128, 128), 128)
        ht_v[:, sl] = h_v[sl, :].T
        return carry

    lax.fori_loop(0, 8, transpose_tile, 0)

    def iteration(i, carry):
        def stage(name, f, count=STEPS):
            s = i - OFF[name]

            @pl.when((s >= 0) & (s < count))
            def _():
                f(s)

        @pl.when(i + LOOKAHEAD < STEPS)
        def _():
            a0(i + LOOKAHEAD)

        stage("A1", a1)
        stage("R0", r0)
        stage("A2", a2)
        stage("R1", r1)
        stage("R2", r2)
        stage("R3", r3)
        stage("A3", a3)
        stage("D1", d1)
        stage("D2A", lambda s: d2a(), 1)
        stage("R4", r4)
        stage("E", e0, 4)
        stage("D2B", lambda s: d2b(), 1)
        return carry

    lax.fori_loop(0, ITERS, iteration, 0)

    def finish(s):
        for k in range(13):
            ag(k, s).wait_send()
        for k in range(12):
            rs(k, s).wait_send()
        core_copy(s).wait_send()
        save_f(s).wait()

    each(STEPS, finish)
    each(6, lambda s: x_copy(s).wait_send())
    zh_copy.wait_send()

    def finish_e(e):
        save_e(e, 0).wait()
        save_e(e, 1).wait()

    each(4, finish_e)
    save_d.wait()


def body(gate_pre, up_pre, down_weight, grad_out):
    replica_rows, ff = gate_pre.shape
    rows, width = grad_out.shape
    scale = 1.0 / math.sqrt(replica_rows * lax.axis_size("dp"))
    vmem, dma = pltpu.VMEM, pltpu.SemaphoreType.DMA
    anywhere = pl.BlockSpec(memory_space=pl.ANY)
    return pl.pallas_call(
        functools.partial(kernel, scale),
        out_shape=(
            jax.ShapeDtypeStruct((rows, width), BF16),
            jax.ShapeDtypeStruct((replica_rows, ff), BF16),
            jax.ShapeDtypeStruct((replica_rows, ff), BF16),
            jax.ShapeDtypeStruct((ff, width // 16), F32),
        ),
        in_specs=[anywhere] * 4,
        out_specs=[anywhere] * 4,
        scratch_shapes=[
            vmem((replica_rows, ff), BF16),
            vmem((replica_rows, ff), BF16),
            vmem((STEPS, ff, WIDTH), BF16),
            vmem((replica_rows, ff), BF16),
            vmem((ff, replica_rows), BF16),
            vmem((STEPS, 8, ROWS, WIDTH), BF16),
            vmem((STEPS, 8, ROWS, WIDTH), BF16),
            vmem((replica_rows, ff), F32),
            vmem((STEPS, 3, RB, WIDTH), BF16),
            vmem((STEPS, 2, RA, HALF), BF16),
            vmem((STEPS, 2, ROWS, HALF), BF16),
            vmem((STEPS, 2, RA, WIDTH), BF16),
            vmem((STEPS, 2, ROWS, WIDTH), BF16),
            vmem((STEPS, 1, ROWS, WIDTH), BF16),
            vmem((STEPS, ff, HALF), BF16),
            vmem((STEPS, ff, HALF), BF16),
            vmem((STEPS, ff, HALF), BF16),
            vmem((6, ff, HALF), BF16),
            vmem((ff, HALF), BF16),
            vmem((ff, HALF), BF16),
            vmem((ff, HALF), F32),
            dma((13, STEPS)), dma((13, STEPS)),
            dma((12, STEPS)), dma((12, STEPS)),
            dma((STEPS,)), dma((STEPS,)),
            dma((6,)), dma((6,)),
            dma, dma,
            dma((STEPS,)), dma((STEPS,)), dma((2,)),
            dma((STEPS,)), dma((2, 4)), dma,
        ],
        compiler_params=pltpu.CompilerParams(
            collective_id=0, has_side_effects=True, vmem_limit_bytes=60 * 1024 * 1024
        ),
        cost_estimate=pl.CostEstimate(
            flops=6 * replica_rows * ff * width, bytes_accessed=20_000_000, transcendentals=2_000_000
        ),
    )(gate_pre, up_pre, down_weight, grad_out)


def solution(mesh):
    return jax.shard_map(
        body,
        mesh=mesh,
        in_specs=(
            P("dp", "tensor"),
            P("dp", "tensor"),
            P("tensor", None),
            P(("dp", "tensor"), None),
        ),
        out_specs=(
            P(("dp", "tensor"), None),
            P("dp", "tensor"),
            P("dp", "tensor"),
            P("tensor", "dp"),
        ),
        check_vma=False,
    )
```

time: 313 us -> 139 us (0.44)
  waiting for transfers between devices: 250 us -> 0 us
  Pallas kernels: 0 us -> 130 us
  matrix products: 44.7 us -> 0 us
  between operations: 13.7 us -> 0.65 us
  local copies, waits for them, and re-layouts: 1.24 us -> 7.33 us
    reduce_scatter x2 -> x0, waiting for transfers between devices: 153 us -> none  [the longest x1 92.5 us: body(): lax.psum_scatter(jnp.dot(hidden_rows, down_weight, preferred_element_type...]
    pallas_call x0 -> x1, Pallas kernels: none -> 130 us  [body(): pl.pallas_call(functools.partial(kernel, scale), out_shape=(jax.ShapeDtyp...]
    all_gather x1 -> x0, waiting for transfers between devices: 96.2 us -> none  [body(): piece = lax.all_gather(grad_out, 'tensor', axis=0, tiled=True)]
    dot_general x3 -> x0, matrix products: 44.7 us -> none  [the longest x1 17.1 us: body(): jnp.einsum('td,fd->tf', piece, down_weight, preferred_element_type=jnp.fl...]
    unnamed x2 -> x10, local copies, waits for them, and re-layouts: 1.24 us -> 7.33 us
  transfers between devices with their start and end apart: 3 -> 0, of which waited for: 3 -> 0; matrix products, arithmetic and copies ran while one was open for 11% -> 0% of each run, Pallas kernels for 0% -> 0%
where the time goes in v1:
time: 139 us; the launch traced here: 138 us
  Pallas kernels  130 us (94%)
  local copies, waits for them, and re-layouts  7.33 us (5%)
    pallas_call x1, Pallas kernels, body(): pl.pallas_call(functools.partial(kernel, scale), out_shape=(jax.ShapeDtyp...  130 us
    unnamed x10, local copies, waits for them, and re-layouts  7.33 us

profile of v1, /device:TPU:0, one launch (start us, length us, event | category | flops | bytes accessed | tf_op | source)
XLA Modules:
  0.0 138.4 jit_solution(5361876918932074775)
XLA Ops:
  0.6 130.4 %shard_map.75 = (bf16[128,4096]{1,0:T(8,128)(2,1)}, bf16[1024,896]{1,0:T(8,128)(2,1)}, bf16[1024,896]{1,0:T(8,128)(2,1)}, f32[896,256]{1,0:T(8,128)}) custom-call(bf16[1024,896]{1,0:T(8,128)(2,1)} %gate_hbm.1, bf16[1024,896]{1,0:T(8,128)(2,1)} %up_hbm.1, bf16[896,4096]{1,0:T(8,128)(2,1)} %w_hbm.1, bf16[128,4096]{1,0:T(8,128)(2,1)} %g_hbm.1), custom_call_target="tpu_custom_call" | custom-call | flops 22548578304 | bytes 20000000 | tf_op jit(solution)/shard_map/pallas_call | solution.py:413
  131.0 0.0 copy-start.1
  131.0 2.4 %copy.12 = bf16[128,4096]{1,0:T(8,128)(2,1)} copy(bf16[128,4096]{1,0:T(8,128)(2,1)} %get-tuple-element.8) | data formatting | bytes 2097152
  133.4 0.0 copy-done.1
  133.5 0.0 copy-start
  133.5 1.2 copy.13
  134.7 0.9 copy-done
  135.6 0.0 copy-start.2
  135.6 1.2 copy.14
  136.8 0.6 copy-done.2
  137.4 0.9 copy.15
Async XLA Ops:
  131.0 2.4 %copy-start.1 = (bf16[1024,896]{1,0:T(8,128)(2,1)S(1)}, bf16[1024,896]{1,0:T(8,128)(2,1)}, u32[]{:S(2)}) copy-start(bf16[1024,896]{1,0:T(8,128)(2,1)} %get-tuple-element.9) | copy-start | bytes 5505028
  133.5 2.2 %copy-start = (bf16[1024,896]{1,0:T(8,128)(2,1)S(1)}, bf16[1024,896]{1,0:T(8,128)(2,1)}, u32[]{:S(2)}) copy-start(bf16[1024,896]{1,0:T(8,128)(2,1)} %get-tuple-element.10) | copy-start | bytes 5505028
  135.6 1.8 %copy-start.2 = (f32[896,256]{1,0:T(8,128)S(1)}, f32[896,256]{1,0:T(8,128)}, u32[]{:S(2)}) copy-start(f32[896,256]{1,0:T(8,128)} %get-tuple-element.11) | copy-start | bytes 2752516

commit v2 on v1

--- a/solution.py
+++ b/solution.py
@@ -16,12 +16,14 @@
 WIDTH = 512
 HALF = 256
 ROWS = 128
-RA = 80
-RB = ROWS - RA
+RA = 48
+RB = 32
+RC = 48
+RAB = RA + RB
 FF = 896
 
 LOOKAHEAD = 3
-OFF = dict(A1=0, A2=1, A3=2, D1=3, R0=0, R1=1, R2=4, R3=5, R4=6, E=10, D2A=10, D2B=12)
+OFF = dict(A1=0, HX=1, A2=1, A3=2, D1=3, R0=1, R1=2, R2=4, R3=5, R4=6, GX=9, GR=11, E=10, D2A=10, D2B=12)
 ITERS = 14
 
 
@@ -43,8 +45,9 @@
     f_out, gg_out, gu_out, gd_out,
     gate_v, up_v, w_v, h_v, ht_v, gb, p, hg,
     rz1, rho, rhw, rfo, rfw, rz2,
+    hx, gs, gr,
     cs, ck, cr, xr, zs, zr, gd_v,
-    ag_s, ag_r, rs_s, rs_r, c_s, c_r, x_s, x_r, zh_s, zh_r,
+    ag_s, ag_r, rs_s, rs_r, c_s, c_r, x_s, x_r, zh_s, zh_r, sw_s, sw_r,
     ld_g, ld_w, ld_a, st_f, st_e, st_d,
 ):
     dp = lax.axis_index("dp")
@@ -57,12 +60,13 @@
     to_yp, to_ym, to_z = (dp, own + yp), (dp, own + ym), (dp, other + y)
     to_core = (x * 4 + zh * 2 + (1 - core), te)
     to_zh = (x * 4 + (1 - zh) * 2 + core, te)
+    to_zc = (x * 4 + (1 - zh) * 2 + core, other + y)
 
     def to_x(d):
         return (((x + d) % 4) * 4 + zh * 2 + core, te)
 
     def column(s):
-        j = 2 * ((x + 1 + s // 2) % 4) + (s + 1 + zh) % 2
+        j = 2 * ((x + 1 + s // 2) % 4) + s % 2
         return pl.ds(pl.multiple_of(j * WIDTH, WIDTH), WIDTH)
 
     def load_g(s):
@@ -87,9 +91,9 @@
     each(STEPS, lambda s: load_w(s).start())
 
     barrier = pltpu.get_barrier_semaphore()
-    for device in (to_yp, to_ym, to_z, to_core, to_zh, to_x(1), to_x(2), to_x(3)):
+    for device in (to_yp, to_ym, to_z, to_zc, to_core, to_zh, to_x(1), to_x(2), to_x(3)):
         pl.semaphore_signal(barrier, inc=1, device_id=device, device_id_type=MESH)
-    pl.semaphore_wait(barrier, 8)
+    pl.semaphore_wait(barrier, 9)
 
     def remote(src, dst, send, recv, device):
         return pltpu.make_async_remote_copy(
@@ -97,11 +101,12 @@
             device_id=device, device_id_type=MESH,
         )
 
-    ROW_ALL, ROW_A, ROW_B = pl.ds(0, ROWS), pl.ds(0, RA), pl.ds(RA, RB)
+    ROW_ALL, ROW_A, ROW_B, ROW_C = pl.ds(0, ROWS), pl.ds(0, RA), pl.ds(RA, RB), pl.ds(RAB, RC)
+    ROW_AB, ROW_BC = pl.ds(0, RAB), pl.ds(RA, RB + RC)
     COL_ALL, COL_0, COL_1 = pl.ds(0, WIDTH), pl.ds(0, HALF), pl.ds(HALF, HALF)
 
     gather = (
-        (own + y, other + y, ROW_ALL, COL_ALL, to_z),
+        (own + y, other + y, ROW_AB, COL_ALL, to_z),
         (own + y, own + ym, ROW_ALL, COL_ALL, to_yp),
         (own + y, own + yp, ROW_ALL, COL_ALL, to_ym),
         (other + y, other + ym, ROW_A, COL_ALL, to_yp),
@@ -114,6 +119,11 @@
         (other + ym, other + y2, ROW_A, COL_1, to_yp),
         (own + y2, other + y2, ROW_B, COL_0, to_z),
         (own + y2, other + y2, ROW_B, COL_1, to_z),
+        (own + y, other + y, ROW_C, COL_ALL, to_zc),
+        (own + yp, other + yp, ROW_C, COL_ALL, to_zc),
+        (own + ym, other + ym, ROW_C, COL_ALL, to_zc),
+        (own + y2, other + y2, ROW_C, COL_0, to_zc),
+        (own + y2, other + y2, ROW_C, COL_1, to_zc),
     )
 
     def ag(k, s, arriving=False):
@@ -127,24 +137,31 @@
     def ag_wait(k, s):
         ag(k, s, True).wait_recv()
 
+    HEAD_B, TAIL_C, ALL = pl.ds(0, RB), pl.ds(RB, RC), slice(None)
     reduction = (
-        (other + yp, ROW_B, COL_ALL, rz1, 0, to_z),
-        (other + ym, ROW_B, COL_ALL, rz1, 1, to_z),
-        (other + y2, ROW_B, COL_ALL, rz1, 2, to_z),
-        (other + y2, ROW_A, COL_0, rho, 0, to_yp),
-        (other + y2, ROW_A, COL_1, rho, 1, to_ym),
-        (own + y2, ROW_ALL, COL_0, rhw, 0, to_yp),
-        (own + y2, ROW_ALL, COL_1, rhw, 1, to_ym),
-        (other + yp, ROW_A, COL_ALL, rfo, 0, to_yp),
-        (other + ym, ROW_A, COL_ALL, rfo, 1, to_ym),
-        (own + yp, ROW_ALL, COL_ALL, rfw, 0, to_yp),
-        (own + ym, ROW_ALL, COL_ALL, rfw, 1, to_ym),
-        (other + y, ROW_ALL, COL_ALL, rz2, 0, to_z),
+        (other + yp, ROW_B, COL_ALL, rz1, 0, HEAD_B, to_z),
+        (other + ym, ROW_B, COL_ALL, rz1, 1, HEAD_B, to_z),
+        (other + y2, ROW_B, COL_ALL, rz1, 2, HEAD_B, to_z),
+        (other + y2, ROW_A, COL_0, rho, 0, ALL, to_yp),
+        (other + y2, ROW_A, COL_1, rho, 1, ALL, to_ym),
+        (own + y2, ROW_ALL, COL_0, rhw, 0, ALL, to_yp),
+        (own + y2, ROW_ALL, COL_1, rhw, 1, ALL, to_ym),
+        (other + yp, ROW_A, COL_ALL, rfo, 0, ALL, to_yp),
+        (other + ym, ROW_A, COL_ALL, rfo, 1, ALL, to_ym),
+        (own + yp, ROW_ALL, COL_ALL, rfw, 0, ALL, to_yp),
+        (own + ym, ROW_ALL, COL_ALL, rfw, 1, ALL, to_ym),
+        (other + y, ROW_AB, COL_ALL, rz2, 0, ROW_AB, to_z),
+        (other + yp, ROW_C, COL_ALL, rz1, 0, TAIL_C, to_zc),
+        (other + ym, ROW_C, COL_ALL, rz1, 1, TAIL_C, to_zc),
+        (other + y2, ROW_C, COL_ALL, rz1, 2, TAIL_C, to_zc),
+        (other + y, ROW_C, COL_ALL, rz2, 0, ROW_C, to_zc),
     )
 
     def rs(k, s):
-        slot, rows, cols, land, index, device = reduction[k]
-        return remote(p.at[s, slot, rows, cols], land.at[s, index], rs_s.at[k, s], rs_r.at[k, s], device)
+        slot, rows, cols, land, index, part, device = reduction[k]
+        return remote(
+            p.at[s, slot, rows, cols], land.at[s, index, part, :], rs_s.at[k, s], rs_r.at[k, s], device
+        )
 
     def rs_send(k, s):
         rs(k, s).start()
@@ -159,10 +176,13 @@
         return remote(ck.at[s], xr.at[s], x_s.at[s], x_r.at[s], to_x(1 + s // 2))
 
     zh_copy = remote(zs, zr, zh_s, zh_r, to_zh)
+    swapped = h_v.at[pl.ds(other, 4), ROW_C, :]
+    h_swap = remote(swapped, hx, sw_s.at[0], sw_r.at[0], to_zh)
+    grad_swap = remote(gs, gr, sw_s.at[1], sw_r.at[1], to_zh)
 
     def a0(s):
         load_g(s).wait()
-        for k in (1, 2, 0):
+        for k in (1, 2, 0, 13):
             ag_send(k, s)
 
     def a1(s):
@@ -172,9 +192,11 @@
         ag_wait(2, s)
         ag_send(5, s)
         ag_send(7, s)
+        ag_send(14, s)
         ag_wait(1, s)
         ag_send(6, s)
         ag_send(8, s)
+        ag_send(15, s)
 
     def a2(s):
         ag_wait(4, s)
@@ -183,11 +205,13 @@
         ag_send(10, s)
         ag_wait(5, s)
         ag_send(11, s)
+        ag_send(16, s)
         ag_wait(6, s)
         ag_send(12, s)
+        ag_send(17, s)
 
     def a3(s):
-        for k in range(7, 13):
+        for k in range(7, 18):
             ag_wait(k, s)
 
         def weight_half(side, dst):
@@ -207,19 +231,19 @@
         weight_half(core, ck)
 
         def tile(t, carry):
-            rows = pl.ds(pl.multiple_of(t * 512, 512), 512)
-            block = gb[s, pl.ds(t * 4, 4)].reshape(512, WIDTH)
+            rows = pl.ds(t * 4, 4)
+            block = gb[s, rows].reshape(512, WIDTH)
             product = lax.dot_general(
                 block, w_v[s], (((1,), (1,)), ((), ())), preferred_element_type=F32
-            )
+            ).reshape(4, ROWS, FF)
 
             @pl.when(s == 0)
             def _():
-                hg[rows, :] = product
+                hg[rows] = product
 
             @pl.when(s > 0)
             def _():
-                hg[rows, :] += product
+                hg[rows] += product
 
             return carry
 
@@ -234,14 +258,14 @@
             x_copy(s).start()
 
     def d2a():
-        for k in (0, 2, 4):
+        for k in range(6):
             x_copy(k).wait_recv()
 
         def tile(t, carry):
             sl = pl.ds(pl.multiple_of(t * 16, 16), 16)
-            total = ck[6, sl, :].astype(F32)
+            total = ck[7 - zh, sl, :].astype(F32)
             for k in (0, 2, 4):
-                total += xr[k, sl, :].astype(F32)
+                total += xr[k + 1 - zh, sl, :].astype(F32)
             zs[sl, :] = total.astype(BF16)
             return carry
 
@@ -251,15 +275,13 @@
     save_d = pltpu.make_async_copy(gd_v, gd_out, st_d)
 
     def d2b():
-        for k in (1, 3, 5):
-            x_copy(k).wait_recv()
         zh_copy.wait_recv()
 
         def tile(t, carry):
             sl = pl.ds(pl.multiple_of(t * 16, 16), 16)
-            total = ck[7, sl, :].astype(F32) + zr[sl, :].astype(F32)
-            for k in (1, 3, 5):
-                total += xr[k, sl, :].astype(F32)
+            total = ck[6 + zh, sl, :].astype(F32) + zr[sl, :].astype(F32)
+            for k in (0, 2, 4):
+                total += xr[k + zh, sl, :].astype(F32)
             gd_v[sl, :] = total
             return carry
 
@@ -270,19 +292,22 @@
         load_w(s).wait()
 
         def tile(t, carry):
-            rows = pl.ds(pl.multiple_of(t * 512, 512), 512)
-            product = jnp.dot(h_v[rows, :], w_v[s], preferred_element_type=F32)
-            p[s, pl.ds(t * 4, 4)] = product.astype(BF16).reshape(4, ROWS, WIDTH)
+            rows = pl.ds(t * 4, 4)
+            product = jnp.dot(
+                h_v[rows].reshape(512, FF), w_v[s], preferred_element_type=F32
+            )
+            p[s, rows] = product.astype(BF16).reshape(4, ROWS, WIDTH)
             return carry
 
         lax.fori_loop(0, 2, tile, 0)
-        for k in (0, 1, 2, 3, 4):
+        for k in (0, 12, 1, 13, 2, 14, 3, 4):
             rs_send(k, s)
 
     def r1(s):
         for k, slot in ((2, own + y2), (0, own + yp), (1, own + ym)):
             rs_wait(k, s)
-            add_rows(p.at[s, slot, ROW_B, :], [rz1.at[s, k]], RB)
+            rs_wait(k + 12, s)
+            add_rows(p.at[s, slot, ROW_BC, :], [rz1.at[s, k]], RB + RC)
             if k == 2:
                 rs_send(5, s)
                 rs_send(6, s)
@@ -304,6 +329,7 @@
     def r3(s):
         rs_wait(7, s)
         rs_wait(8, s)
+        rs_send(15, s)
         add_rows(p.at[s, other + y, ROW_A, :], [rfo.at[s, 0], rfo.at[s, 1]], RA)
         rs_send(11, s)
 
@@ -311,22 +337,27 @@
         return pltpu.make_async_copy(p.at[s, te], f_out.at[:, column(s)], st_f.at[s])
 
     def r4(s):
-        for k in (9, 10, 11):
+        for k in (9, 10, 11, 15):
             rs_wait(k, s)
         add_rows(p.at[s, te], [rfw.at[s, 0], rfw.at[s, 1], rz2.at[s, 0]], ROWS)
         save_f(s).start()
 
     def save_e(e, which):
-        rows = pl.ds(pl.multiple_of(e * 256, 256), 256)
+        first = jnp.where(e < 2, own, other) + (e % 2) * 2
+        rows = pl.ds(pl.multiple_of(first * ROWS, 2 * ROWS), 2 * ROWS)
         src, dst = ((gate_v, gg_out), (up_v, gu_out))[which]
         return pltpu.make_async_copy(src.at[rows, :], dst.at[rows, :], st_e.at[which, e])
 
     def e0(e):
-        def tile(t, carry):
-            sl = pl.ds(pl.multiple_of(e * 256 + t * 16, 16), 16)
+        first = jnp.where(e < 2, own, other) + (e % 2) * 2
+
+        def tile(t, carry):
+            slot = first + t // 8
+            row = pl.multiple_of((t % 8) * 16, 16)
+            sl = pl.ds(pl.multiple_of(slot * ROWS + row, 16), 16)
             g = gate_v[sl, :].astype(F32)
             u = up_v[sl, :].astype(F32)
-            grad = hg[sl, :]
+            grad = hg[slot, pl.ds(row, 16), :]
             s = jax.nn.sigmoid(g)
             gate_v[sl, :] = (grad * u * s * (1.0 + g * (1.0 - s))).astype(BF16)
             up_v[sl, :] = (grad * (g * s)).astype(BF16)
@@ -336,25 +367,63 @@
         save_e(e, 0).start()
         save_e(e, 1).start()
 
+    def swap_tiles(f):
+        def tile(t, carry):
+            row = pl.multiple_of((t % 3) * 16, 16)
+            f(t // 3, pl.ds(row, 16), pl.ds(RAB + row, 16))
+            return carry
+
+        lax.fori_loop(0, 4 * (RC // 16), tile, 0)
+
+    def gx():
+        def move(k, part, row):
+            gs[k, part, :] = hg[other + k, row, :].astype(BF16)
+
+        swap_tiles(move)
+        grad_swap.start()
+
+    def gr_stage():
+        grad_swap.wait_recv()
+
+        def move(k, part, row):
+            hg[other + k, row, :] = gr[k, part, :].astype(F32)
+
+        swap_tiles(move)
+
+    def hidden_rows(slot, row, count):
+        def tile(t, carry):
+            start = pl.multiple_of(row + t * 16, 16)
+            sl = pl.ds(pl.multiple_of(slot * ROWS + start, 16), 16)
+            g = gate_v[sl, :].astype(F32)
+            u = up_v[sl, :].astype(F32)
+            h_v[slot, pl.ds(start, 16), :] = (g * jax.nn.sigmoid(g) * u).astype(BF16)
+            return carry
+
+        lax.fori_loop(0, count // 16, tile, 0)
+
+    def hx_stage():
+        h_swap.wait_send()
+        h_swap.wait_recv()
+
+        def move(k, part, row):
+            h_v[other + k, row, :] = hx[k, part, :]
+
+        swap_tiles(move)
+
+        def transpose_tile(t, carry):
+            ht_v[:, pl.ds(pl.multiple_of(t * ROWS, ROWS), ROWS)] = h_v[t].T
+            return carry
+
+        lax.fori_loop(0, 8, transpose_tile, 0)
+
     each(LOOKAHEAD, a0)
     load_gate.wait()
     load_up.wait()
 
-    def hidden_tile(t, carry):
-        sl = pl.ds(pl.multiple_of(t * 16, 16), 16)
-        g = gate_v[sl, :].astype(F32)
-        u = up_v[sl, :].astype(F32)
-        h_v[sl, :] = (g * jax.nn.sigmoid(g) * u).astype(BF16)
-        return carry
-
-    lax.fori_loop(0, 64, hidden_tile, 0)
-
-    def transpose_tile(t, carry):
-        sl = pl.ds(pl.multiple_of(t * 128, 128), 128)
-        ht_v[:, sl] = h_v[sl, :].T
-        return carry
-
-    lax.fori_loop(0, 8, transpose_tile, 0)
+    each(4, lambda k: hidden_rows(other + k, RAB, RC))
+    h_swap.start()
+    each(4, lambda k: hidden_rows(own + k, 0, ROWS))
+    each(4, lambda k: hidden_rows(other + k, 0, RAB))
 
     def iteration(i, carry):
         def stage(name, f, count=STEPS):
@@ -369,15 +438,18 @@
             a0(i + LOOKAHEAD)
 
         stage("A1", a1)
+        stage("A2", a2)
+        stage("HX", lambda s: hx_stage(), 1)
         stage("R0", r0)
-        stage("A2", a2)
         stage("R1", r1)
         stage("R2", r2)
         stage("R3", r3)
         stage("A3", a3)
+        stage("GX", lambda s: gx(), 1)
         stage("D1", d1)
         stage("D2A", lambda s: d2a(), 1)
         stage("R4", r4)
+        stage("GR", lambda s: gr_stage(), 1)
         stage("E", e0, 4)
         stage("D2B", lambda s: d2b(), 1)
         return carry
@@ -385,9 +457,9 @@
     lax.fori_loop(0, ITERS, iteration, 0)
 
     def finish(s):
-        for k in range(13):
+        for k in range(18):
             ag(k, s).wait_send()
-        for k in range(12):
+        for k in range(16):
             rs(k, s).wait_send()
         core_copy(s).wait_send()
         save_f(s).wait()
@@ -395,6 +467,7 @@
     each(STEPS, finish)
     each(6, lambda s: x_copy(s).wait_send())
     zh_copy.wait_send()
+    grad_swap.wait_send()
 
     def finish_e(e):
         save_e(e, 0).wait()
@@ -402,6 +475,43 @@
 
     each(4, finish_e)
     save_d.wait()
+
+
+PIECES = 4
+
+
+def settle_kernel(a0, a1, a2, a3, b0, b1, b2, b3, v0, v1, v2, v3, load_sem, save_sem):
+    pieces = []
+    for k, (src, mid, dst) in enumerate(((a1, v1, b1), (a2, v2, b2), (a0, v0, b0), (a3, v3, b3))):
+        count = src.shape[0] // PIECES
+        for part in range(PIECES):
+            rows = pl.ds(part * count, count)
+            n = k * PIECES + part
+            pieces.append((
+                pltpu.make_async_copy(src.at[rows, :], mid.at[rows, :], load_sem.at[n]),
+                pltpu.make_async_copy(mid.at[rows, :], dst.at[rows, :], save_sem.at[n]),
+            ))
+    for load, _ in pieces:
+        load.start()
+    for load, save in pieces:
+        load.wait()
+        save.start()
+    for _, save in pieces:
+        save.wait()
+
+
+def settle(outs):
+    anywhere = pl.BlockSpec(memory_space=pl.ANY)
+    return pl.pallas_call(
+        settle_kernel,
+        out_shape=tuple(jax.ShapeDtypeStruct(o.shape, o.dtype) for o in outs),
+        in_specs=[anywhere] * 4,
+        out_specs=[anywhere] * 4,
+        scratch_shapes=[pltpu.VMEM(o.shape, o.dtype) for o in outs]
+        + [pltpu.SemaphoreType.DMA((4 * PIECES,))] * 2,
+        compiler_params=pltpu.CompilerParams(vmem_limit_bytes=60 * 1024 * 1024),
+        cost_estimate=pl.CostEstimate(flops=0, bytes_accessed=11_000_000, transcendentals=0),
+    )(*outs)
 
 
 def body(gate_pre, up_pre, down_weight, grad_out):
@@ -410,7 +520,7 @@
     scale = 1.0 / math.sqrt(replica_rows * lax.axis_size("dp"))
     vmem, dma = pltpu.VMEM, pltpu.SemaphoreType.DMA
     anywhere = pl.BlockSpec(memory_space=pl.ANY)
-    return pl.pallas_call(
+    outs = pl.pallas_call(
         functools.partial(kernel, scale),
         out_shape=(
             jax.ShapeDtypeStruct((rows, width), BF16),
@@ -424,17 +534,20 @@
             vmem((replica_rows, ff), BF16),
             vmem((replica_rows, ff), BF16),
             vmem((STEPS, ff, WIDTH), BF16),
-            vmem((replica_rows, ff), BF16),
+            vmem((8, ROWS, ff), BF16),
             vmem((ff, replica_rows), BF16),
             vmem((STEPS, 8, ROWS, WIDTH), BF16),
             vmem((STEPS, 8, ROWS, WIDTH), BF16),
-            vmem((replica_rows, ff), F32),
-            vmem((STEPS, 3, RB, WIDTH), BF16),
+            vmem((8, ROWS, ff), F32),
+            vmem((STEPS, 3, RB + RC, WIDTH), BF16),
             vmem((STEPS, 2, RA, HALF), BF16),
             vmem((STEPS, 2, ROWS, HALF), BF16),
             vmem((STEPS, 2, RA, WIDTH), BF16),
             vmem((STEPS, 2, ROWS, WIDTH), BF16),
             vmem((STEPS, 1, ROWS, WIDTH), BF16),
+            vmem((4, RC, ff), BF16),
+            vmem((4, RC, ff), BF16),
+            vmem((4, RC, ff), BF16),
             vmem((STEPS, ff, HALF), BF16),
             vmem((STEPS, ff, HALF), BF16),
             vmem((STEPS, ff, HALF), BF16),
@@ -442,11 +555,12 @@
             vmem((ff, HALF), BF16),
             vmem((ff, HALF), BF16),
             vmem((ff, HALF), F32),
-            dma((13, STEPS)), dma((13, STEPS)),
-            dma((12, STEPS)), dma((12, STEPS)),
+            dma((18, STEPS)), dma((18, STEPS)),
+            dma((16, STEPS)), dma((16, STEPS)),
             dma((STEPS,)), dma((STEPS,)),
             dma((6,)), dma((6,)),
             dma, dma,
+            dma((2,)), dma((2,)),
             dma((STEPS,)), dma((STEPS,)), dma((2,)),
             dma((STEPS,)), dma((2, 4)), dma,
         ],
@@ -457,6 +571,7 @@
             flops=6 * replica_rows * ff * width, bytes_accessed=20_000_000, transcendentals=2_000_000
         ),
     )(gate_pre, up_pre, down_weight, grad_out)
+    return settle(outs)
 
 
 def solution(mesh):

time: 139 us -> 126 us (0.906)
  local copies, waits for them, and re-layouts: 7.33 us -> 0 us
  Pallas kernels: 130 us -> 125 us
    pallas_call x1, Pallas kernels: 130 us -> 120 us  [body(): pl.pallas_call(functools.partial(kernel, scale), out_shape=(jax.ShapeDtyp...]
    unnamed x10 -> x0, local copies, waits for them, and re-layouts: 7.33 us -> none
    pallas_call x0 -> x1, Pallas kernels: none -> 5.16 us  [settle(): pl.pallas_call(settle_kernel, out_shape=tuple((jax.ShapeDtypeStruct(o.sha...]
where the time goes in v2:
time: 126 us
  Pallas kernels  125 us (99%)
    pallas_call x1, Pallas kernels, body(): pl.pallas_call(functools.partial(kernel, scale), out_shape=(jax.ShapeDtyp...  120 us
    pallas_call x1, Pallas kernels, settle(): pl.pallas_call(settle_kernel, out_shape=tuple((jax.ShapeDtypeStruct(o.sha...  5.16 us

profile of v2, /device:TPU:0, one launch (start us, length us, event | category | flops | bytes accessed | tf_op | source)
XLA Modules:
  0.0 125.9 jit_solution(13369841927054656272)
XLA Ops:
  0.6 120.1 %shard_map.75 = (bf16[128,4096]{1,0:T(8,128)(2,1)}, bf16[1024,896]{1,0:T(8,128)(2,1)}, bf16[1024,896]{1,0:T(8,128)(2,1)}, f32[896,256]{1,0:T(8,128)}) custom-call(bf16[1024,896]{1,0:T(8,128)(2,1)} %gate_hbm.1, bf16[1024,896]{1,0:T(8,128)(2,1)} %up_hbm.1, bf16[896,4096]{1,0:T(8,128)(2,1)} %w_hbm.1, bf16[128,4096]{1,0:T(8,128)(2,1)} %g_hbm.1), custom_call_target="tpu_custom_call" | custom-call | flops 22548578304 | bytes 20000000 | tf_op jit(solution)/shard_map/pallas_call | solution.py:523
  120.7 5.2 %shard_map.76 = (bf16[128,4096]{1,0:T(8,128)(2,1)}, bf16[1024,896]{1,0:T(8,128)(2,1)}, bf16[1024,896]{1,0:T(8,128)(2,1)}, f32[896,256]{1,0:T(8,128)}) custom-call(bf16[128,4096]{1,0:T(8,128)(2,1)} %get-tuple-element.8.a0, bf16[1024,896]{1,0:T(8,128)(2,1)} %get-tuple-element.9.a1, bf16[1024,896]{1,0:T(8,128)(2,1)} %get-tuple-element.10.a2, ...), custom_call_target="tpu_custom_call" | custom-call | bytes 11000000 | tf_op jit(solution)/shard_map/pallas_call | solution.py:505

commit v3 on v2

--- a/solution.py
+++ b/solution.py
@@ -11,6 +11,9 @@
 MESH = pl.DeviceIdType.MESH
 F32 = jnp.float32
 BF16 = jnp.bfloat16
+
+GATHER_GROUP = (0, 1, 1, 2, 2, 3, 3) + (4,) * 11
+REDUCE_GROUP = (0, 0, 0, 1, 1, 2, 2, 3, 3, 4, 4, 4, 0, 0, 0, 4)
 
 STEPS = 8
 WIDTH = 512
@@ -65,15 +68,18 @@
     def to_x(d):
         return (((x + d) % 4) * 4 + zh * 2 + core, te)
 
+    def distance(s):
+        return jnp.where(s < 4, 1 + 2 * (s % 2), jnp.where(s < 6, 2, 0))
+
     def column(s):
-        j = 2 * ((x + 1 + s // 2) % 4) + s % 2
+        j = 2 * ((x + distance(s)) % 4) + jnp.where(s < 4, s // 2, s % 2)
         return pl.ds(pl.multiple_of(j * WIDTH, WIDTH), WIDTH)
 
     def load_g(s):
-        return pltpu.make_async_copy(g_hbm.at[:, column(s)], gb.at[s, te], ld_g.at[s])
+        return pltpu.make_async_copy(g_hbm.at[:, column(s)], gb.at[s, te], ld_g)
 
     def load_w(s):
-        return pltpu.make_async_copy(w_hbm.at[:, column(s)], w_v.at[s], ld_w.at[s])
+        return pltpu.make_async_copy(w_hbm.at[:, column(s)], w_v.at[s], ld_w)
 
     load_gate = pltpu.make_async_copy(gate_hbm, gate_v, ld_a.at[0])
     load_up = pltpu.make_async_copy(up_hbm, up_v, ld_a.at[1])
@@ -126,16 +132,26 @@
         (own + y2, other + y2, ROW_C, COL_1, to_zc),
     )
 
-    def ag(k, s, arriving=False):
-        leaves, arrives, rows, cols, device = gather[k]
-        ref = gb.at[s, arrives if arriving else leaves, rows, cols]
-        return remote(ref, ref, ag_s.at[k, s], ag_r.at[k, s], device)
-
     def ag_send(k, s):
-        ag(k, s).start()
-
-    def ag_wait(k, s):
-        ag(k, s, True).wait_recv()
+        leaves, _, rows, cols, device = gather[k]
+        ref = gb.at[s, leaves, rows, cols]
+        remote(ref, ref, ag_s.at[s], ag_r.at[GATHER_GROUP[k], s], device).start()
+
+    def arrived(ref, sem):
+        remote(ref, ref, sem, sem, to_z).wait_recv()
+
+    def left(ref, sem):
+        remote(ref, ref, sem, sem, to_z).wait_send()
+
+    def ag_wait(group, s):
+        ref = (
+            gb.at[s, 0, ROW_AB, :],
+            gb.at[s, pl.ds(0, 2)],
+            gb.at[s, pl.ds(0, 2), ROW_A, :],
+            gb.at[s, 0],
+            gb.at[s, pl.ds(0, 3), pl.ds(0, 112), :],
+        )[group]
+        arrived(ref, ag_r.at[group, s])
 
     HEAD_B, TAIL_C, ALL = pl.ds(0, RB), pl.ds(RB, RC), slice(None)
     reduction = (
@@ -157,23 +173,28 @@
         (other + y, ROW_C, COL_ALL, rz2, 0, ROW_C, to_zc),
     )
 
-    def rs(k, s):
+    def rs_send(k, s):
         slot, rows, cols, land, index, part, device = reduction[k]
-        return remote(
-            p.at[s, slot, rows, cols], land.at[s, index, part, :], rs_s.at[k, s], rs_r.at[k, s], device
-        )
-
-    def rs_send(k, s):
-        rs(k, s).start()
-
-    def rs_wait(k, s):
-        rs(k, s).wait_recv()
+        remote(
+            p.at[s, slot, rows, cols], land.at[s, index, part, :],
+            rs_s.at[s], rs_r.at[REDUCE_GROUP[k], s], device,
+        ).start()
+
+    def rs_wait(group, s):
+        ref = (
+            p.at[s, pl.ds(0, 3), ROW_AB, :],
+            p.at[s, 0, ROW_A, :],
+            p.at[s, 0],
+            p.at[s, pl.ds(0, 2), ROW_A, :],
+            p.at[s, pl.ds(0, 3)],
+        )[group]
+        arrived(ref, rs_r.at[group, s])
 
     def core_copy(s):
-        return remote(cs.at[s], cr.at[s], c_s.at[s], c_r.at[s], to_core)
+        return remote(cs.at[s], cr.at[s], c_s, c_r.at[s], to_core)
 
     def x_copy(s):
-        return remote(ck.at[s], xr.at[s], x_s.at[s], x_r.at[s], to_x(1 + s // 2))
+        return remote(ck.at[s], xr.at[s], x_s, x_r, to_x(distance(s)))
 
     zh_copy = remote(zs, zr, zh_s, zh_r, to_zh)
     swapped = h_v.at[pl.ds(other, 4), ROW_C, :]
@@ -181,7 +202,6 @@
     grad_swap = remote(gs, gr, sw_s.at[1], sw_r.at[1], to_zh)
 
     def a0(s):
-        load_g(s).wait()
         for k in (1, 2, 0, 13):
             ag_send(k, s)
 
@@ -189,30 +209,20 @@
         ag_wait(0, s)
         ag_send(3, s)
         ag_send(4, s)
+        ag_wait(1, s)
+        for k in (5, 6, 7, 8, 14, 15):
+            ag_send(k, s)
+
+    def a2(s):
         ag_wait(2, s)
-        ag_send(5, s)
-        ag_send(7, s)
-        ag_send(14, s)
-        ag_wait(1, s)
-        ag_send(6, s)
-        ag_send(8, s)
-        ag_send(15, s)
-
-    def a2(s):
+        ag_send(9, s)
+        ag_send(10, s)
+        ag_wait(3, s)
+        for k in (11, 12, 16, 17):
+            ag_send(k, s)
+
+    def a3(s):
         ag_wait(4, s)
-        ag_send(9, s)
-        ag_wait(3, s)
-        ag_send(10, s)
-        ag_wait(5, s)
-        ag_send(11, s)
-        ag_send(16, s)
-        ag_wait(6, s)
-        ag_send(12, s)
-        ag_send(17, s)
-
-    def a3(s):
-        for k in range(7, 18):
-            ag_wait(k, s)
 
         def weight_half(side, dst):
             cols = pl.ds(pl.multiple_of(side * HALF, HALF), HALF)
@@ -258,14 +268,13 @@
             x_copy(s).start()
 
     def d2a():
-        for k in range(6):
-            x_copy(k).wait_recv()
+        arrived(xr, x_r)
 
         def tile(t, carry):
             sl = pl.ds(pl.multiple_of(t * 16, 16), 16)
             total = ck[7 - zh, sl, :].astype(F32)
-            for k in (0, 2, 4):
-                total += xr[k + 1 - zh, sl, :].astype(F32)
+            for k, d in ((0, 2), (1, 2), (4, 1)):
+                total += xr[k + (1 - zh) * d, sl, :].astype(F32)
             zs[sl, :] = total.astype(BF16)
             return carry
 
@@ -280,8 +289,8 @@
         def tile(t, carry):
             sl = pl.ds(pl.multiple_of(t * 16, 16), 16)
             total = ck[6 + zh, sl, :].astype(F32) + zr[sl, :].astype(F32)
-            for k in (0, 2, 4):
-                total += xr[k + zh, sl, :].astype(F32)
+            for k, d in ((0, 2), (1, 2), (4, 1)):
+                total += xr[k + zh * d, sl, :].astype(F32)
             gd_v[sl, :] = total
             return carry
 
@@ -289,8 +298,6 @@
         save_d.start()
 
     def r0(s):
-        load_w(s).wait()
-
         def tile(t, carry):
             rows = pl.ds(t * 4, 4)
             product = jnp.dot(
@@ -304,41 +311,36 @@
             rs_send(k, s)
 
     def r1(s):
+        rs_wait(0, s)
         for k, slot in ((2, own + y2), (0, own + yp), (1, own + ym)):
-            rs_wait(k, s)
-            rs_wait(k + 12, s)
             add_rows(p.at[s, slot, ROW_BC, :], [rz1.at[s, k]], RB + RC)
             if k == 2:
                 rs_send(5, s)
                 rs_send(6, s)
 
     def r2(s):
-        rs_wait(3, s)
+        rs_wait(1, s)
         add_rows(p.at[s, other + yp, ROW_A, COL_0], [rho.at[s, 0]], RA)
         rs_send(7, s)
-        rs_wait(4, s)
         add_rows(p.at[s, other + ym, ROW_A, COL_1], [rho.at[s, 1]], RA)
         rs_send(8, s)
-        rs_wait(5, s)
+        rs_wait(2, s)
         add_rows(p.at[s, own + yp, ROW_ALL, COL_0], [rhw.at[s, 0]], ROWS)
         rs_send(9, s)
-        rs_wait(6, s)
         add_rows(p.at[s, own + ym, ROW_ALL, COL_1], [rhw.at[s, 1]], ROWS)
         rs_send(10, s)
 
     def r3(s):
-        rs_wait(7, s)
-        rs_wait(8, s)
         rs_send(15, s)
+        rs_wait(3, s)
         add_rows(p.at[s, other + y, ROW_A, :], [rfo.at[s, 0], rfo.at[s, 1]], RA)
         rs_send(11, s)
 
     def save_f(s):
-        return pltpu.make_async_copy(p.at[s, te], f_out.at[:, column(s)], st_f.at[s])
+        return pltpu.make_async_copy(p.at[s, te], f_out.at[:, column(s)], st_f)
 
     def r4(s):
-        for k in (9, 10, 11, 15):
-            rs_wait(k, s)
+        rs_wait(4, s)
         add_rows(p.at[s, te], [rfw.at[s, 0], rfw.at[s, 1], rz2.at[s, 0]], ROWS)
         save_f(s).start()
 
@@ -346,7 +348,7 @@
         first = jnp.where(e < 2, own, other) + (e % 2) * 2
         rows = pl.ds(pl.multiple_of(first * ROWS, 2 * ROWS), 2 * ROWS)
         src, dst = ((gate_v, gg_out), (up_v, gu_out))[which]
-        return pltpu.make_async_copy(src.at[rows, :], dst.at[rows, :], st_e.at[which, e])
+        return pltpu.make_async_copy(src.at[rows, :], dst.at[rows, :], st_e.at[which])
 
     def e0(e):
         first = jnp.where(e < 2, own, other) + (e % 2) * 2
@@ -402,6 +404,7 @@
         lax.fori_loop(0, count // 16, tile, 0)
 
     def hx_stage():
+        pltpu.make_async_copy(w_v, w_v, ld_w).wait()
         h_swap.wait_send()
         h_swap.wait_recv()
 
@@ -416,6 +419,7 @@
 
         lax.fori_loop(0, 8, transpose_tile, 0)
 
+    pltpu.make_async_copy(gb.at[:, te], gb.at[:, te], ld_g).wait()
     each(LOOKAHEAD, a0)
     load_gate.wait()
     load_up.wait()
@@ -457,23 +461,17 @@
     lax.fori_loop(0, ITERS, iteration, 0)
 
     def finish(s):
-        for k in range(18):
-            ag(k, s).wait_send()
-        for k in range(16):
-            rs(k, s).wait_send()
-        core_copy(s).wait_send()
-        save_f(s).wait()
+        left(gb.at[s, pl.ds(0, 7)], ag_s.at[s])
+        left(p.at[s, pl.ds(0, 7)], rs_s.at[s])
 
     each(STEPS, finish)
-    each(6, lambda s: x_copy(s).wait_send())
+    left(cs, c_s)
+    left(xr, x_s)
     zh_copy.wait_send()
     grad_swap.wait_send()
-
-    def finish_e(e):
-        save_e(e, 0).wait()
-        save_e(e, 1).wait()
-
-    each(4, finish_e)
+    pltpu.make_async_copy(p.at[:, te], p.at[:, te], st_f).wait()
+    pltpu.make_async_copy(gate_v, gg_out, st_e.at[0]).wait()
+    pltpu.make_async_copy(up_v, gu_out, st_e.at[1]).wait()
     save_d.wait()
 
 
@@ -555,14 +553,14 @@
             vmem((ff, HALF), BF16),
             vmem((ff, HALF), BF16),
             vmem((ff, HALF), F32),
-            dma((18, STEPS)), dma((18, STEPS)),
-            dma((16, STEPS)), dma((16, STEPS)),
-            dma((STEPS,)), dma((STEPS,)),
-            dma((6,)), dma((6,)),
+            dma((STEPS,)), dma((5, STEPS)),
+            dma((STEPS,)), dma((5, STEPS)),
+            dma, dma((STEPS,)),
+            dma, dma,
             dma, dma,
             dma((2,)), dma((2,)),
-            dma((STEPS,)), dma((STEPS,)), dma((2,)),
-            dma((STEPS,)), dma((2, 4)), dma,
+            dma, dma, dma((2,)),
+            dma, dma((2,)), dma,
         ],
         compiler_params=pltpu.CompilerParams(
             collective_id=0, has_side_effects=True, vmem_limit_bytes=60 * 1024 * 1024

time: 126 us -> 122 us (0.968)
  Pallas kernels: 125 us -> 121 us
    pallas_call x1, Pallas kernels: 120 us -> 116 us  [body(): pl.pallas_call(functools.partial(kernel, scale), out_shape=(jax.ShapeDtyp...]
where the time goes in v3:
time: 122 us
  Pallas kernels  121 us (99%)
    pallas_call x1, Pallas kernels, body(): pl.pallas_call(functools.partial(kernel, scale), out_shape=(jax.ShapeDtyp...  116 us
    pallas_call x1, Pallas kernels, settle(): pl.pallas_call(settle_kernel, out_shape=tuple((jax.ShapeDtypeStruct(o.sha...  5.16 us

profile of v3, /device:TPU:0, one launch (start us, length us, event | category | flops | bytes accessed | tf_op | source)
XLA Modules:
  0.0 121.6 jit_solution(1320236711455219249)
XLA Ops:
  0.6 115.8 %shard_map.75 = (bf16[128,4096]{1,0:T(8,128)(2,1)}, bf16[1024,896]{1,0:T(8,128)(2,1)}, bf16[1024,896]{1,0:T(8,128)(2,1)}, f32[896,256]{1,0:T(8,128)}) custom-call(bf16[1024,896]{1,0:T(8,128)(2,1)} %gate_hbm.1, bf16[1024,896]{1,0:T(8,128)(2,1)} %up_hbm.1, bf16[896,4096]{1,0:T(8,128)(2,1)} %w_hbm.1, bf16[128,4096]{1,0:T(8,128)(2,1)} %g_hbm.1), custom_call_target="tpu_custom_call" | custom-call | flops 22548578304 | bytes 20000000 | tf_op jit(solution)/shard_map/pallas_call | solution.py:521
  116.5 5.2 %shard_map.76 = (bf16[128,4096]{1,0:T(8,128)(2,1)}, bf16[1024,896]{1,0:T(8,128)(2,1)}, bf16[1024,896]{1,0:T(8,128)(2,1)}, f32[896,256]{1,0:T(8,128)}) custom-call(bf16[128,4096]{1,0:T(8,128)(2,1)} %get-tuple-element.8.a0, bf16[1024,896]{1,0:T(8,128)(2,1)} %get-tuple-element.9.a1, bf16[1024,896]{1,0:T(8,128)(2,1)} %get-tuple-element.10.a2, ...), custom_call_target="tpu_custom_call" | custom-call | bytes 11000000 | tf_op jit(solution)/shard_map/pallas_call | solution.py:503

commit v4 on v3

--- a/solution.py
+++ b/solution.py
@@ -26,8 +26,8 @@
 FF = 896
 
 LOOKAHEAD = 3
-OFF = dict(A1=0, HX=1, A2=1, A3=2, D1=3, R0=1, R1=2, R2=4, R3=5, R4=6, GX=9, GR=11, E=10, D2A=10, D2B=12)
-ITERS = 14
+OFF = dict(A1=0, HX=1, A2=1, A3=2, D1=3, R0=2, R1=4, R2=6, R3=8, R4=10, GX=9, GR=11, E=10, D2A=11, D2B=16)
+ITERS = 18
 
 
 def add_rows(dst, srcs, rows):

time: 122 us -> 115 us (0.943)
  Pallas kernels: 121 us -> 114 us
    pallas_call x1, Pallas kernels: 116 us -> 109 us  [body(): pl.pallas_call(functools.partial(kernel, scale), out_shape=(jax.ShapeDtyp...]
where the time goes in v4:
time: 115 us
  Pallas kernels  114 us (99%)
    pallas_call x1, Pallas kernels, body(): pl.pallas_call(functools.partial(kernel, scale), out_shape=(jax.ShapeDtyp...  109 us
    pallas_call x1, Pallas kernels, settle(): pl.pallas_call(settle_kernel, out_shape=tuple((jax.ShapeDtypeStruct(o.sha...  5.16 us

profile of v4, /device:TPU:0, one launch (start us, length us, event | category | flops | bytes accessed | tf_op | source)
XLA Modules:
  0.0 114.8 jit_solution(16442507436710567633)
XLA Ops:
  0.6 109.0 %shard_map.75 = (bf16[128,4096]{1,0:T(8,128)(2,1)}, bf16[1024,896]{1,0:T(8,128)(2,1)}, bf16[1024,896]{1,0:T(8,128)(2,1)}, f32[896,256]{1,0:T(8,128)}) custom-call(bf16[1024,896]{1,0:T(8,128)(2,1)} %gate_hbm.1, bf16[1024,896]{1,0:T(8,128)(2,1)} %up_hbm.1, bf16[896,4096]{1,0:T(8,128)(2,1)} %w_hbm.1, bf16[128,4096]{1,0:T(8,128)(2,1)} %g_hbm.1), custom_call_target="tpu_custom_call" | custom-call | flops 22548578304 | bytes 20000000 | tf_op jit(solution)/shard_map/pallas_call | solution.py:521
  109.7 5.2 %shard_map.76 = (bf16[128,4096]{1,0:T(8,128)(2,1)}, bf16[1024,896]{1,0:T(8,128)(2,1)}, bf16[1024,896]{1,0:T(8,128)(2,1)}, f32[896,256]{1,0:T(8,128)}) custom-call(bf16[128,4096]{1,0:T(8,128)(2,1)} %get-tuple-element.8.a0, bf16[1024,896]{1,0:T(8,128)(2,1)} %get-tuple-element.9.a1, bf16[1024,896]{1,0:T(8,128)(2,1)} %get-tuple-element.10.a2, ...), custom_call_target="tpu_custom_call" | custom-call | bytes 11000000 | tf_op jit(solution)/shard_map/pallas_call | solution.py:503

commit v5 on v4

--- a/solution.py
+++ b/solution.py
@@ -26,7 +26,7 @@
 FF = 896
 
 LOOKAHEAD = 3
-OFF = dict(A1=0, HX=1, A2=1, A3=2, D1=3, R0=2, R1=4, R2=6, R3=8, R4=10, GX=9, GR=11, E=10, D2A=11, D2B=16)
+OFF = dict(A1=0, HX=1, A2=1, A3=2, D1=3, R0=2, R1=4, R2=6, R3=8, R4=10, GX=9, GR=11, E=10, D2A=12, D2B=17)
 ITERS = 18
 
 
@@ -437,12 +437,13 @@
             def _():
                 f(s)
 
+        stage("A1", a1)
+        stage("A2", a2)
+
         @pl.when(i + LOOKAHEAD < STEPS)
         def _():
             a0(i + LOOKAHEAD)
 
-        stage("A1", a1)
-        stage("A2", a2)
         stage("HX", lambda s: hx_stage(), 1)
         stage("R0", r0)
         stage("R1", r1)
@@ -475,7 +476,7 @@
     save_d.wait()
 
 
-PIECES = 4
+PIECES = 2
 
 
 def settle_kernel(a0, a1, a2, a3, b0, b1, b2, b3, v0, v1, v2, v3, load_sem, save_sem):

time: 115 us -> 113 us (0.983)
  Pallas kernels: 114 us -> 112 us
    pallas_call x1, Pallas kernels: 109 us -> 108 us  [body(): pl.pallas_call(functools.partial(kernel, scale), out_shape=(jax.ShapeDtyp...]
where the time goes in v5:
time: 113 us
  Pallas kernels  112 us (99%)
    pallas_call x1, Pallas kernels, body(): pl.pallas_call(functools.partial(kernel, scale), out_shape=(jax.ShapeDtyp...  108 us
    pallas_call x1, Pallas kernels, settle(): pl.pallas_call(settle_kernel, out_shape=tuple((jax.ShapeDtypeStruct(o.sha...  4.72 us

profile of v5, /device:TPU:0, one launch (start us, length us, event | category | flops | bytes accessed | tf_op | source)
XLA Modules:
  0.0 113.0 jit_solution(2779997818402751646)
XLA Ops:
  0.6 107.7 %shard_map.75 = (bf16[128,4096]{1,0:T(8,128)(2,1)}, bf16[1024,896]{1,0:T(8,128)(2,1)}, bf16[1024,896]{1,0:T(8,128)(2,1)}, f32[896,256]{1,0:T(8,128)}) custom-call(bf16[1024,896]{1,0:T(8,128)(2,1)} %gate_hbm.1, bf16[1024,896]{1,0:T(8,128)(2,1)} %up_hbm.1, bf16[896,4096]{1,0:T(8,128)(2,1)} %w_hbm.1, bf16[128,4096]{1,0:T(8,128)(2,1)} %g_hbm.1), custom_call_target="tpu_custom_call" | custom-call | flops 22548578304 | bytes 20000000 | tf_op jit(solution)/shard_map/pallas_call | solution.py:522
  108.3 4.7 %shard_map.76 = (bf16[128,4096]{1,0:T(8,128)(2,1)}, bf16[1024,896]{1,0:T(8,128)(2,1)}, bf16[1024,896]{1,0:T(8,128)(2,1)}, f32[896,256]{1,0:T(8,128)}) custom-call(bf16[128,4096]{1,0:T(8,128)(2,1)} %get-tuple-element.8.a0, bf16[1024,896]{1,0:T(8,128)(2,1)} %get-tuple-element.9.a1, bf16[1024,896]{1,0:T(8,128)(2,1)} %get-tuple-element.10.a2, ...), custom_call_target="tpu_custom_call" | custom-call | bytes 11000000 | tf_op jit(solution)/shard_map/pallas_call | solution.py:504

commit v6 on v5

--- a/solution.py
+++ b/solution.py
@@ -202,7 +202,7 @@
     grad_swap = remote(gs, gr, sw_s.at[1], sw_r.at[1], to_zh)
 
     def a0(s):
-        for k in (1, 2, 0, 13):
+        for k in (0, 1, 2, 13):
             ag_send(k, s)
 
     def a1(s):

time: 113 us -> 113 us (level)
  no operation moved by 1% of the time
where the time goes in v6:
time: 113 us
  Pallas kernels  112 us (99%)
    pallas_call x1, Pallas kernels, body(): pl.pallas_call(functools.partial(kernel, scale), out_shape=(jax.ShapeDtyp...  108 us
    pallas_call x1, Pallas kernels, settle(): pl.pallas_call(settle_kernel, out_shape=tuple((jax.ShapeDtypeStruct(o.sha...  4.72 us

profile of v6, /device:TPU:0, one launch (start us, length us, event | category | flops | bytes accessed | tf_op | source)
XLA Modules:
  0.0 113.0 jit_solution(714115735337447816)
XLA Ops:
  0.6 107.7 %shard_map.75 = (bf16[128,4096]{1,0:T(8,128)(2,1)}, bf16[1024,896]{1,0:T(8,128)(2,1)}, bf16[1024,896]{1,0:T(8,128)(2,1)}, f32[896,256]{1,0:T(8,128)}) custom-call(bf16[1024,896]{1,0:T(8,128)(2,1)} %gate_hbm.1, bf16[1024,896]{1,0:T(8,128)(2,1)} %up_hbm.1, bf16[896,4096]{1,0:T(8,128)(2,1)} %w_hbm.1, bf16[128,4096]{1,0:T(8,128)(2,1)} %g_hbm.1), custom_call_target="tpu_custom_call" | custom-call | flops 22548578304 | bytes 20000000 | tf_op jit(solution)/shard_map/pallas_call | solution.py:522
  108.3 4.7 %shard_map.76 = (bf16[128,4096]{1,0:T(8,128)(2,1)}, bf16[1024,896]{1,0:T(8,128)(2,1)}, bf16[1024,896]{1,0:T(8,128)(2,1)}, f32[896,256]{1,0:T(8,128)}) custom-call(bf16[128,4096]{1,0:T(8,128)(2,1)} %get-tuple-element.8.a0, bf16[1024,896]{1,0:T(8,128)(2,1)} %get-tuple-element.9.a1, bf16[1024,896]{1,0:T(8,128)(2,1)} %get-tuple-element.10.a2, ...), custom_call_target="tpu_custom_call" | custom-call | bytes 11000000 | tf_op jit(solution)/shard_map/pallas_call | solution.py:504
